TPU v7x, 32 devices: a whole 2x2x4 slice. The times are simulated.
32 devices in a mesh: row: 4 (over x, core), col: 8 (over z, y).
Axes of the slice: x: 2, y: 2, z: 4, core: 2. Of those that a mesh axis runs over, the one named last changes fastest.
Arguments:
- vectors: float32 [8192, 1024], P('row', 'col'), may hold values from -6 to 6
- reflectors: float32 [4, 32, 256, 128], P('row', 'col'), may hold values from -0.375 to 0.375
- wy_factors: float32 [4, 32, 128, 128], P('row', 'col'), may hold values from -1 to 3, as said below
- block_slots: int32 [4, 4, 4], P('row'), may hold values from 0 to 31, as said below
- offsets: int32 [4, 4, 3], P('row'), may hold values from 0 to 1792
Outputs:
- transformed: float32 [8192, 1024], P('row', 'col')
Inputs may be any that keep to these rules, and one draw needn't show every extreme that they name: `wy_factors`: upper triangular; diagonal entries between 1.2 and 2.8. `block_slots`: the entries of one row group are distinct; slot k of every group lies on the col index k // 4. The border entry of the last row group is not read.
All inputs are finite; a program needn't handle non-finite values.
Results may differ from a plain program's by a relative error of at most 0.00026.
Values sent between devices are 32-bit elements; how exact they have to be, the bound alone decides.
No kernel may reach another device: no remote copies, remote signals or barrier semaphores. Data moves between devices by JAX's collectives and lax.ppermute only.
A program may use at most 64 MiB of HBM per device.

v0:
```python
import jax
import jax.numpy as jnp
from jax import lax
from jax.sharding import PartitionSpec as P


def spread(block, axis, source):
    block = jnp.where(lax.axis_index(axis) == source, block, jnp.zeros_like(block))
    return lax.psum(block, axis)


def shifted(block, axis, distance):
    devices = range(lax.axis_size(axis))
    route = [(i - distance, i) for i in devices if i - distance in devices]
    return lax.ppermute(block, axis, route)


def reflect(block, basis, factor):
    best = lax.Precision.HIGHEST
    coeffs = jnp.dot(basis.T, block, precision=best, preferred_element_type=jnp.float32)
    scaled = jnp.dot(factor, coeffs, precision=best, preferred_element_type=jnp.float32)
    return block - jnp.dot(basis, scaled, precision=best, preferred_element_type=jnp.float32)


def fetch_block(block_slots, reflectors, wy_factors, step_no, block_no):
    hold_count = reflectors.shape[1]
    slot_id = block_slots[0, step_no, block_no]
    local_slot = slot_id % hold_count
    root_col = slot_id // hold_count
    parcel = (
        lax.dynamic_index_in_dim(reflectors[0], local_slot, 0, False),
        lax.dynamic_index_in_dim(wy_factors[0], local_slot, 0, False),
    )
    return (spread(parcel[0], "col", root_col), spread(parcel[1], "col", root_col))


def advance(
    current, incoming, beneath, step_no, group_index, group_total_count, bases, factors, offsets
):
    edge_rows = beneath.shape[0]
    total_rows = current.shape[0]
    inner_count = offsets.shape[2]
    head = jnp.where(group_index > 0, incoming, current[:edge_rows])
    current = lax.dynamic_update_slice_in_dim(current, head, 0, 0)
    step_bases = lax.dynamic_index_in_dim(bases, step_no, 0, False)
    step_factors = lax.dynamic_index_in_dim(factors, step_no, 0, False)
    step_offsets = lax.dynamic_index_in_dim(offsets[0], step_no, 0, False)
    for block_no in range(inner_count):
        start = step_offsets[block_no]
        block = lax.dynamic_slice_in_dim(current, start, 2 * edge_rows, 0)
        block = reflect(block, step_bases[block_no], step_factors[block_no])
        current = lax.dynamic_update_slice_in_dim(current, block, start, 0)
    bottom = current[total_rows - edge_rows :]
    joined = reflect(
        jnp.concatenate([bottom, beneath], 0), step_bases[inner_count], step_factors[inner_count]
    )
    has_below = group_index < group_total_count - 1
    tail = jnp.where(has_below, joined[:edge_rows], bottom)
    current = lax.dynamic_update_slice_in_dim(current, tail, total_rows - edge_rows, 0)
    return (current, joined[edge_rows:])


def per_device(vectors, reflectors, wy_factors, block_slots, offsets):
    group_total_count = lax.axis_size("row")
    group_index = lax.axis_index("row")
    step_count = offsets.shape[1]
    inner_count = offsets.shape[2]
    edge_rows = reflectors.shape[3]
    column_count = vectors.shape[1]
    base_list = []
    factor_list = []
    for step_no in range(step_count):
        for block_no in range(inner_count + 1):
            basis, factor = fetch_block(block_slots, reflectors, wy_factors, step_no, block_no)
            base_list.append(basis)
            factor_list.append(factor)
    bases = jnp.stack(base_list).reshape((step_count, inner_count + 1) + base_list[0].shape)
    factors = jnp.stack(factor_list).reshape((step_count, inner_count + 1) + factor_list[0].shape)
    empty_rows = jnp.zeros((edge_rows, column_count), jnp.float32)
    current = vectors

    def wave_tick(tick_no, carry):
        current, incoming = carry
        beneath = shifted(current[:edge_rows], "row", -1)
        time_lag = tick_no - group_index
        step_now = time_lag // 2
        active = (time_lag >= 0) & (time_lag % 2 == 0) & (step_now < step_count)
        step_safe = jnp.clip(step_now, 0, step_count - 1)
        current, outgoing = lax.cond(
            active,
            lambda operands: advance(
                operands[0],
                operands[1],
                beneath,
                step_safe,
                group_index,
                group_total_count,
                bases,
                factors,
                offsets,
            ),
            lambda operands: (operands[0], jnp.zeros_like(operands[1])),
            (current, incoming),
        )
        incoming = shifted(outgoing, "row", 1)
        return (current, incoming)

    current, incoming = lax.fori_loop(
        0, group_total_count + 2 * step_count - 2, wave_tick, (current, empty_rows)
    )
    return current


def solution(mesh):
    in_specs = (
        P("row", "col"),
        P("row", "col", None, None),
        P("row", "col", None, None),
        P("row", None, None),
        P("row", None, None),
    )
    out_specs = P("row", "col")
    return jax.shard_map(
        per_device, mesh=mesh, in_specs=in_specs, out_specs=out_specs, check_vma=False
    )
```

profile of v0, /device:TPU:3, one launch (start us, length us, event | category | flops | bytes accessed | tf_op | source)
XLA Modules:
  0.0 467.4 jit_solution(14436373289902219683)
XLA Ops:
  48.8 1.0 select_bitcast_fusion
  51.6 144.5 %all-reduce.3.cloned.1.call-done = (f32[1,256,128]{2,1,0:T(8,128)}, f32[1,256,128]{2,1,0:T(8,128)}, f32[1,256,128]{2,1,0:T(8,128)}, f32[1,256,128]{2,1,0:T(8,128...) async-done(((f32[1,256,128]{2,1,0:T(8,128)}, ...) | async-done | bytes 3145744 | tf_op jit(solution)/shard_map/psum | solution.py:9
  210.9 248.8 %while.20 = (s32[]{:T(128)}, f32[2048,128]{1,0:T(8,128)S(1)}, f32[128,128]{1,0:T(8,128)S(1)}, s32[]{:T(128)}, s32[1,4,3]{1,0,2:T(1,128)S(1)}, /*index=5*/f32[4,4...) while((s32[]{:T(128)}, f32[2048,128]{1,0:T(8,128)S(1)}, ...), condition=%wide.region_35.36_spmd, body=%wide.region_32.35_spmd.sunk | while | flops 503545888 | bytes 6030164 | solution.py:108
  210.9 2.7 collective-permute-start
  214.5 1.3 collective-permute-start.1
  215.8 2.4 collective-permute-done.1
  218.2 4.9 %collective-permute-start = (f32[128,128]{1,0:T(8,128)S(1)}, f32[128,128]{1,0:T(8,128)S(1)}, u32[]{:S(2)}, u32[]{:S(2)}) collective-permute-start(f32[128,128]{1,0:T(8,128)S(1)} %slice.171), channel_id=1, source_target_pairs={{8,0},{16,8},{24,16},{9,1},{17,9},{25,17},{10,2},{18,10},{26,18},{... | collective-permute-start | bytes 196616 | tf_op jit(solution)/shard_map/while/body/eval_jaxpr/ppermute | solution.py:15
  224.0 1.3 collective-permute-start.1
  225.2 14.6 %collective-permute-done.1 = f32[128,128]{1,0:T(8,128)S(1)} collective-permute-done((f32[128,128]{1,0:T(8,128)S(1)}, f32[128,128]{1,0:T(8,128)S(1)}, u32[]{:S(2)}, u32[]{:S(2)}) %collective-permute-start.1) | collective-permute-done | bytes 65568 | tf_op jit(solution)/shard_map/while/body/eval_jaxpr/ppermute | solution.py:15
  239.9 20.7 %collective-permute-start = (f32[128,128]{1,0:T(8,128)S(1)}, f32[128,128]{1,0:T(8,128)S(1)}, u32[]{:S(2)}, u32[]{:S(2)}) collective-permute-start(f32[128,128]{1,0:T(8,128)S(1)} %slice.171), channel_id=1, source_target_pairs={{8,0},{16,8},{24,16},{9,1},{17,9},{25,17},{10,2},{18,10},{26,18},{... | collective-permute-start | bytes 196616 | tf_op jit(solution)/shard_map/while/body/eval_jaxpr/ppermute | solution.py:15
  261.5 1.3 collective-permute-start.1
  262.8 18.6 %collective-permute-done.1 = f32[128,128]{1,0:T(8,128)S(1)} collective-permute-done((f32[128,128]{1,0:T(8,128)S(1)}, f32[128,128]{1,0:T(8,128)S(1)}, u32[]{:S(2)}, u32[]{:S(2)}) %collective-permute-start.1) | collective-permute-done | bytes 65568 | tf_op jit(solution)/shard_map/while/body/eval_jaxpr/ppermute | solution.py:15
  281.3 4.8 %collective-permute-start = (f32[128,128]{1,0:T(8,128)S(1)}, f32[128,128]{1,0:T(8,128)S(1)}, u32[]{:S(2)}, u32[]{:S(2)}) collective-permute-start(f32[128,128]{1,0:T(8,128)S(1)} %slice.171), channel_id=1, source_target_pairs={{8,0},{16,8},{24,16},{9,1},{17,9},{25,17},{10,2},{18,10},{26,18},{... | collective-permute-start | bytes 196616 | tf_op jit(solution)/shard_map/while/body/eval_jaxpr/ppermute | solution.py:15
  287.1 16.2 %conditional.2 = (f32[2048,128]{1,0:T(8,128)S(1)}, f32[128,128]{1,0:T(8,128)S(1)}) conditional(s32[]{:T(128)} %convert_element_type.11, f32[2048,128]{1,0:T(8,128)S(1)} %get-tuple-element.402, (s32[]{:T(128)}, f32[2048,128]{1,0:T(8,128)S(1)}, f32[128,128]{1,0:T(8,128)S(1)}, s32[]{:T(128)}, s32[1,4,3]{1,0,2:T(1,128)S(1)}, ...), branch_computations={%region_33.33_spmd, %region_34.34_spmd} | conditional | flops 503545856 | bytes 5374306 | solution.py:89
  289.9 1.0 fusion.11
  291.2 1.0 dynamic_update_slice.16
  294.5 1.0 fusion.10
  295.8 1.0 dynamic_update_slice.17
  299.1 1.0 fusion.9
  300.5 1.0 dynamic_update_slice.18
  301.9 1.0 fusion.8
  303.3 1.3 collective-permute-start.1
  304.6 1.8 collective-permute-done.1
  306.4 5.1 %collective-permute-start = (f32[128,128]{1,0:T(8,128)S(1)}, f32[128,128]{1,0:T(8,128)S(1)}, u32[]{:S(2)}, u32[]{:S(2)}) collective-permute-start(f32[128,128]{1,0:T(8,128)S(1)} %slice.171), channel_id=1, source_target_pairs={{8,0},{16,8},{24,16},{9,1},{17,9},{25,17},{10,2},{18,10},{26,18},{... | collective-permute-start | bytes 196616 | tf_op jit(solution)/shard_map/while/body/eval_jaxpr/ppermute | solution.py:15
  312.4 1.3 collective-permute-start.1
  313.7 18.6 %collective-permute-done.1 = f32[128,128]{1,0:T(8,128)S(1)} collective-permute-done((f32[128,128]{1,0:T(8,128)S(1)}, f32[128,128]{1,0:T(8,128)S(1)}, u32[]{:S(2)}, u32[]{:S(2)}) %collective-permute-start.1) | collective-permute-done | bytes 65568 | tf_op jit(solution)/shard_map/while/body/eval_jaxpr/ppermute | solution.py:15
  332.3 4.8 %collective-permute-start = (f32[128,128]{1,0:T(8,128)S(1)}, f32[128,128]{1,0:T(8,128)S(1)}, u32[]{:S(2)}, u32[]{:S(2)}) collective-permute-start(f32[128,128]{1,0:T(8,128)S(1)} %slice.171), channel_id=1, source_target_pairs={{8,0},{16,8},{24,16},{9,1},{17,9},{25,17},{10,2},{18,10},{26,18},{... | collective-permute-start | bytes 196616 | tf_op jit(solution)/shard_map/while/body/eval_jaxpr/ppermute | solution.py:15
  338.0 16.1 %conditional.2 = (f32[2048,128]{1,0:T(8,128)S(1)}, f32[128,128]{1,0:T(8,128)S(1)}) conditional(s32[]{:T(128)} %convert_element_type.11, f32[2048,128]{1,0:T(8,128)S(1)} %get-tuple-element.402, (s32[]{:T(128)}, f32[2048,128]{1,0:T(8,128)S(1)}, f32[128,128]{1,0:T(8,128)S(1)}, s32[]{:T(128)}, s32[1,4,3]{1,0,2:T(1,128)S(1)}, ...), branch_computations={%region_33.33_spmd, %region_34.34_spmd} | conditional | flops 503545856 | bytes 5374306 | solution.py:89
  340.8 1.0 fusion.11
  345.3 1.0 fusion.10
  346.7 1.0 dynamic_update_slice.17
  349.9 1.0 fusion.9
  351.3 1.0 dynamic_update_slice.18
  352.7 1.0 fusion.8
  354.1 1.3 collective-permute-start.1
  355.4 1.8 collective-permute-done.1
  357.2 5.4 %collective-permute-start = (f32[128,128]{1,0:T(8,128)S(1)}, f32[128,128]{1,0:T(8,128)S(1)}, u32[]{:S(2)}, u32[]{:S(2)}) collective-permute-start(f32[128,128]{1,0:T(8,128)S(1)} %slice.171), channel_id=1, source_target_pairs={{8,0},{16,8},{24,16},{9,1},{17,9},{25,17},{10,2},{18,10},{26,18},{... | collective-permute-start | bytes 196616 | tf_op jit(solution)/shard_map/while/body/eval_jaxpr/ppermute | solution.py:15
  363.6 1.3 collective-permute-start.1
  364.8 18.6 %collective-permute-done.1 = f32[128,128]{1,0:T(8,128)S(1)} collective-permute-done((f32[128,128]{1,0:T(8,128)S(1)}, f32[128,128]{1,0:T(8,128)S(1)}, u32[]{:S(2)}, u32[]{:S(2)}) %collective-permute-start.1) | collective-permute-done | bytes 65568 | tf_op jit(solution)/shard_map/while/body/eval_jaxpr/ppermute | solution.py:15
  383.4 4.8 %collective-permute-start = (f32[128,128]{1,0:T(8,128)S(1)}, f32[128,128]{1,0:T(8,128)S(1)}, u32[]{:S(2)}, u32[]{:S(2)}) collective-permute-start(f32[128,128]{1,0:T(8,128)S(1)} %slice.171), channel_id=1, source_target_pairs={{8,0},{16,8},{24,16},{9,1},{17,9},{25,17},{10,2},{18,10},{26,18},{... | collective-permute-start | bytes 196616 | tf_op jit(solution)/shard_map/while/body/eval_jaxpr/ppermute | solution.py:15
  389.1 16.2 %conditional.2 = (f32[2048,128]{1,0:T(8,128)S(1)}, f32[128,128]{1,0:T(8,128)S(1)}) conditional(s32[]{:T(128)} %convert_element_type.11, f32[2048,128]{1,0:T(8,128)S(1)} %get-tuple-element.402, (s32[]{:T(128)}, f32[2048,128]{1,0:T(8,128)S(1)}, f32[128,128]{1,0:T(8,128)S(1)}, s32[]{:T(128)}, s32[1,4,3]{1,0,2:T(1,128)S(1)}, ...), branch_computations={%region_33.33_spmd, %region_34.34_spmd} | conditional | flops 503545856 | bytes 5374306 | solution.py:89
  391.9 1.0 fusion.11
  393.3 1.0 dynamic_update_slice.16
  396.6 1.0 fusion.10
  397.9 1.0 dynamic_update_slice.17
  401.2 1.0 fusion.9
  402.5 1.0 dynamic_update_slice.18
  404.0 1.0 fusion.8
  405.3 1.3 collective-permute-start.1
  406.6 1.8 collective-permute-done.1
  408.5 5.4 %collective-permute-start = (f32[128,128]{1,0:T(8,128)S(1)}, f32[128,128]{1,0:T(8,128)S(1)}, u32[]{:S(2)}, u32[]{:S(2)}) collective-permute-start(f32[128,128]{1,0:T(8,128)S(1)} %slice.171), channel_id=1, source_target_pairs={{8,0},{16,8},{24,16},{9,1},{17,9},{25,17},{10,2},{18,10},{26,18},{... | collective-permute-start | bytes 196616 | tf_op jit(solution)/shard_map/while/body/eval_jaxpr/ppermute | solution.py:15
  414.8 1.3 collective-permute-start.1
  416.1 18.6 %collective-permute-done.1 = f32[128,128]{1,0:T(8,128)S(1)} collective-permute-done((f32[128,128]{1,0:T(8,128)S(1)}, f32[128,128]{1,0:T(8,128)S(1)}, u32[]{:S(2)}, u32[]{:S(2)}) %collective-permute-start.1) | collective-permute-done | bytes 65568 | tf_op jit(solution)/shard_map/while/body/eval_jaxpr/ppermute | solution.py:15
  434.7 4.8 %collective-permute-start = (f32[128,128]{1,0:T(8,128)S(1)}, f32[128,128]{1,0:T(8,128)S(1)}, u32[]{:S(2)}, u32[]{:S(2)}) collective-permute-start(f32[128,128]{1,0:T(8,128)S(1)} %slice.171), channel_id=1, source_target_pairs={{8,0},{16,8},{24,16},{9,1},{17,9},{25,17},{10,2},{18,10},{26,18},{... | collective-permute-start | bytes 196616 | tf_op jit(solution)/shard_map/while/body/eval_jaxpr/ppermute | solution.py:15
  440.4 16.1 %conditional.2 = (f32[2048,128]{1,0:T(8,128)S(1)}, f32[128,128]{1,0:T(8,128)S(1)}) conditional(s32[]{:T(128)} %convert_element_type.11, f32[2048,128]{1,0:T(8,128)S(1)} %get-tuple-element.402, (s32[]{:T(128)}, f32[2048,128]{1,0:T(8,128)S(1)}, f32[128,128]{1,0:T(8,128)S(1)}, s32[]{:T(128)}, s32[1,4,3]{1,0,2:T(1,128)S(1)}, ...), branch_computations={%region_33.33_spmd, %region_34.34_spmd} | conditional | flops 503545856 | bytes 5374306 | solution.py:89
  443.2 1.0 fusion.11
  447.7 1.0 fusion.10
  449.1 1.0 dynamic_update_slice.17
  452.4 1.0 fusion.9
  453.7 1.0 dynamic_update_slice.18
  455.1 1.0 fusion.8
  456.5 1.3 collective-permute-start.1
  457.8 1.8 collective-permute-done.1
  459.6 1.0 copy-done
  (168 shorter events, 42.1 us)
Async XLA Ops:
  6.5 42.2 %copy-start.2 = (f32[1,4,256,128]{3,2,1,0:T(8,128)S(1)}, f32[1,4,256,128]{3,2,1,0:T(8,128)}, u32[]{:S(2)}) copy-start(f32[1,4,256,128]{3,2,1,0:T(8,128)} %param.10) | copy-start | bytes 1572868
  6.5 41.4 %copy-start.3 = (f32[1,4,128,128]{3,2,1,0:T(8,128)S(1)}, f32[1,4,128,128]{3,2,1,0:T(8,128)}, u32[]{:S(2)}) copy-start(f32[1,4,128,128]{3,2,1,0:T(8,128)} %param.11) | copy-start | bytes 786436
  6.5 0.8 copy-start.23
  6.5 189.5 %all-reduce.3.cloned.1.call-start = ((), (), s32[]{:S(2)}) async-start(), calls=%async_computation | async-start | bytes 6291456 | tf_op jit(solution)/shard_map/psum | solution.py:9
  196.1 13.2 %copy-start.21 = (f32[1,128,128]{2,1,0:T(8,128)S(1)}, f32[1,128,128]{2,1,0:T(8,128)}, u32[]{:S(2)}) copy-start(f32[1,128,128]{2,1,0:T(8,128)} %get-tuple-element.283) | copy-start | bytes 196612
  196.1 13.2 %copy-start.20 = (f32[1,128,128]{2,1,0:T(8,128)S(1)}, f32[1,128,128]{2,1,0:T(8,128)}, u32[]{:S(2)}) copy-start(f32[1,128,128]{2,1,0:T(8,128)} %get-tuple-element.284) | copy-start | bytes 196612
  196.1 13.2 %copy-start.19 = (f32[1,256,128]{2,1,0:T(8,128)S(1)}, f32[1,256,128]{2,1,0:T(8,128)}, u32[]{:S(2)}) copy-start(f32[1,256,128]{2,1,0:T(8,128)} %get-tuple-element.254) | copy-start | bytes 393220
  196.1 13.3 %copy-start.18 = (f32[1,256,128]{2,1,0:T(8,128)S(1)}, f32[1,256,128]{2,1,0:T(8,128)}, u32[]{:S(2)}) copy-start(f32[1,256,128]{2,1,0:T(8,128)} %get-tuple-element.255) | copy-start | bytes 393220
  196.1 13.3 %copy-start.17 = (f32[1,256,128]{2,1,0:T(8,128)S(1)}, f32[1,256,128]{2,1,0:T(8,128)}, u32[]{:S(2)}) copy-start(f32[1,256,128]{2,1,0:T(8,128)} %get-tuple-element.256) | copy-start | bytes 393220
  196.1 13.3 %copy-start.16 = (f32[1,256,128]{2,1,0:T(8,128)S(1)}, f32[1,256,128]{2,1,0:T(8,128)}, u32[]{:S(2)}) copy-start(f32[1,256,128]{2,1,0:T(8,128)} %get-tuple-element.257) | copy-start | bytes 393220
  196.1 13.3 %copy-start.15 = (f32[1,256,128]{2,1,0:T(8,128)S(1)}, f32[1,256,128]{2,1,0:T(8,128)}, u32[]{:S(2)}) copy-start(f32[1,256,128]{2,1,0:T(8,128)} %get-tuple-element.258) | copy-start | bytes 393220
  196.1 13.4 %copy-start.14 = (f32[1,256,128]{2,1,0:T(8,128)S(1)}, f32[1,256,128]{2,1,0:T(8,128)}, u32[]{:S(2)}) copy-start(f32[1,256,128]{2,1,0:T(8,128)} %get-tuple-element.259) | copy-start | bytes 393220
  196.1 13.4 %copy-start.13 = (f32[1,256,128]{2,1,0:T(8,128)S(1)}, f32[1,256,128]{2,1,0:T(8,128)}, u32[]{:S(2)}) copy-start(f32[1,256,128]{2,1,0:T(8,128)} %get-tuple-element.260) | copy-start | bytes 393220
  196.1 13.4 %copy-start.12 = (f32[1,256,128]{2,1,0:T(8,128)S(1)}, f32[1,256,128]{2,1,0:T(8,128)}, u32[]{:S(2)}) copy-start(f32[1,256,128]{2,1,0:T(8,128)} %get-tuple-element.261) | copy-start | bytes 393220
  198.0 11.6 %copy-start.11 = (f32[1,256,128]{2,1,0:T(8,128)S(1)}, f32[1,256,128]{2,1,0:T(8,128)}, u32[]{:S(2)}) copy-start(f32[1,256,128]{2,1,0:T(8,128)} %get-tuple-element.262) | copy-start | bytes 393220
  198.9 10.7 %copy-start.10 = (f32[1,256,128]{2,1,0:T(8,128)S(1)}, f32[1,256,128]{2,1,0:T(8,128)}, u32[]{:S(2)}) copy-start(f32[1,256,128]{2,1,0:T(8,128)} %get-tuple-element.263) | copy-start | bytes 393220
  200.6 9.0 %copy-start.9 = (f32[1,256,128]{2,1,0:T(8,128)S(1)}, f32[1,256,128]{2,1,0:T(8,128)}, u32[]{:S(2)}) copy-start(f32[1,256,128]{2,1,0:T(8,128)} %get-tuple-element.264) | copy-start | bytes 393220
  202.3 7.3 %copy-start.8 = (f32[1,256,128]{2,1,0:T(8,128)S(1)}, f32[1,256,128]{2,1,0:T(8,128)}, u32[]{:S(2)}) copy-start(f32[1,256,128]{2,1,0:T(8,128)} %get-tuple-element.265) | copy-start | bytes 393220
  204.1 5.6 %copy-start.7 = (f32[1,256,128]{2,1,0:T(8,128)S(1)}, f32[1,256,128]{2,1,0:T(8,128)}, u32[]{:S(2)}) copy-start(f32[1,256,128]{2,1,0:T(8,128)} %get-tuple-element.266) | copy-start | bytes 393220
  205.8 3.9 copy-start.6
  207.5 2.2 copy-start.5
  209.3 1.6 copy-start.1
  209.3 1.6 copy-start.22
  209.3 1.0 copy-start.4
  210.9 3.6 collective-permute-start
  214.5 3.7 collective-permute-start.1
  218.2 5.8 %collective-permute-start = (f32[128,128]{1,0:T(8,128)S(1)}, f32[128,128]{1,0:T(8,128)S(1)}, u32[]{:S(2)}, u32[]{:S(2)}) collective-permute-start(f32[128,128]{1,0:T(8,128)S(1)} %slice.171), channel_id=1, source_target_pairs={{8,0},{16,8},{24,16},{9,1},{17,9},{25,17},{10,2},{18,10},{26,18},{... | collective-permute-start | bytes 196616 | tf_op jit(solution)/shard_map/while/body/eval_jaxpr/ppermute | solution.py:15
  224.0 15.9 %collective-permute-start.1 = (f32[128,128]{1,0:T(8,128)S(1)}, f32[128,128]{1,0:T(8,128)S(1)}, u32[]{:S(2)}, u32[]{:S(2)}) collective-permute-start(f32[128,128]{1,0:T(8,128)S(1)} %get-tuple-element.384), channel_id=1, source_target_pairs={{0,8},{8,16},{16,24},{1,9},{9,17},{17,25},{2,10},{10,18},{18,26},{... | collective-permute-start | bytes 196616 | tf_op jit(solution)/shard_map/while/body/eval_jaxpr/ppermute | solution.py:15
  239.9 21.6 %collective-permute-start = (f32[128,128]{1,0:T(8,128)S(1)}, f32[128,128]{1,0:T(8,128)S(1)}, u32[]{:S(2)}, u32[]{:S(2)}) collective-permute-start(f32[128,128]{1,0:T(8,128)S(1)} %slice.171), channel_id=1, source_target_pairs={{8,0},{16,8},{24,16},{9,1},{17,9},{25,17},{10,2},{18,10},{26,18},{... | collective-permute-start | bytes 196616 | tf_op jit(solution)/shard_map/while/body/eval_jaxpr/ppermute | solution.py:15
  261.5 19.9 %collective-permute-start.1 = (f32[128,128]{1,0:T(8,128)S(1)}, f32[128,128]{1,0:T(8,128)S(1)}, u32[]{:S(2)}, u32[]{:S(2)}) collective-permute-start(f32[128,128]{1,0:T(8,128)S(1)} %get-tuple-element.384), channel_id=1, source_target_pairs={{0,8},{8,16},{16,24},{1,9},{9,17},{17,25},{2,10},{10,18},{18,26},{... | collective-permute-start | bytes 196616 | tf_op jit(solution)/shard_map/while/body/eval_jaxpr/ppermute | solution.py:15
  281.3 5.7 %collective-permute-start = (f32[128,128]{1,0:T(8,128)S(1)}, f32[128,128]{1,0:T(8,128)S(1)}, u32[]{:S(2)}, u32[]{:S(2)}) collective-permute-start(f32[128,128]{1,0:T(8,128)S(1)} %slice.171), channel_id=1, source_target_pairs={{8,0},{16,8},{24,16},{9,1},{17,9},{25,17},{10,2},{18,10},{26,18},{... | collective-permute-start | bytes 196616 | tf_op jit(solution)/shard_map/while/body/eval_jaxpr/ppermute | solution.py:15
  303.3 3.1 collective-permute-start.1
  306.4 6.0 %collective-permute-start = (f32[128,128]{1,0:T(8,128)S(1)}, f32[128,128]{1,0:T(8,128)S(1)}, u32[]{:S(2)}, u32[]{:S(2)}) collective-permute-start(f32[128,128]{1,0:T(8,128)S(1)} %slice.171), channel_id=1, source_target_pairs={{8,0},{16,8},{24,16},{9,1},{17,9},{25,17},{10,2},{18,10},{26,18},{... | collective-permute-start | bytes 196616 | tf_op jit(solution)/shard_map/while/body/eval_jaxpr/ppermute | solution.py:15
  312.4 19.9 %collective-permute-start.1 = (f32[128,128]{1,0:T(8,128)S(1)}, f32[128,128]{1,0:T(8,128)S(1)}, u32[]{:S(2)}, u32[]{:S(2)}) collective-permute-start(f32[128,128]{1,0:T(8,128)S(1)} %get-tuple-element.384), channel_id=1, source_target_pairs={{0,8},{8,16},{16,24},{1,9},{9,17},{17,25},{2,10},{10,18},{18,26},{... | collective-permute-start | bytes 196616 | tf_op jit(solution)/shard_map/while/body/eval_jaxpr/ppermute | solution.py:15
  332.3 5.7 %collective-permute-start = (f32[128,128]{1,0:T(8,128)S(1)}, f32[128,128]{1,0:T(8,128)S(1)}, u32[]{:S(2)}, u32[]{:S(2)}) collective-permute-start(f32[128,128]{1,0:T(8,128)S(1)} %slice.171), channel_id=1, source_target_pairs={{8,0},{16,8},{24,16},{9,1},{17,9},{25,17},{10,2},{18,10},{26,18},{... | collective-permute-start | bytes 196616 | tf_op jit(solution)/shard_map/while/body/eval_jaxpr/ppermute | solution.py:15
  354.1 3.1 collective-permute-start.1
  357.2 6.3 %collective-permute-start = (f32[128,128]{1,0:T(8,128)S(1)}, f32[128,128]{1,0:T(8,128)S(1)}, u32[]{:S(2)}, u32[]{:S(2)}) collective-permute-start(f32[128,128]{1,0:T(8,128)S(1)} %slice.171), channel_id=1, source_target_pairs={{8,0},{16,8},{24,16},{9,1},{17,9},{25,17},{10,2},{18,10},{26,18},{... | collective-permute-start | bytes 196616 | tf_op jit(solution)/shard_map/while/body/eval_jaxpr/ppermute | solution.py:15
  363.6 19.9 %collective-permute-start.1 = (f32[128,128]{1,0:T(8,128)S(1)}, f32[128,128]{1,0:T(8,128)S(1)}, u32[]{:S(2)}, u32[]{:S(2)}) collective-permute-start(f32[128,128]{1,0:T(8,128)S(1)} %get-tuple-element.384), channel_id=1, source_target_pairs={{0,8},{8,16},{16,24},{1,9},{9,17},{17,25},{2,10},{10,18},{18,26},{... | collective-permute-start | bytes 196616 | tf_op jit(solution)/shard_map/while/body/eval_jaxpr/ppermute | solution.py:15
  383.4 5.7 %collective-permute-start = (f32[128,128]{1,0:T(8,128)S(1)}, f32[128,128]{1,0:T(8,128)S(1)}, u32[]{:S(2)}, u32[]{:S(2)}) collective-permute-start(f32[128,128]{1,0:T(8,128)S(1)} %slice.171), channel_id=1, source_target_pairs={{8,0},{16,8},{24,16},{9,1},{17,9},{25,17},{10,2},{18,10},{26,18},{... | collective-permute-start | bytes 196616 | tf_op jit(solution)/shard_map/while/body/eval_jaxpr/ppermute | solution.py:15
  405.3 3.1 collective-permute-start.1
  408.5 6.3 %collective-permute-start = (f32[128,128]{1,0:T(8,128)S(1)}, f32[128,128]{1,0:T(8,128)S(1)}, u32[]{:S(2)}, u32[]{:S(2)}) collective-permute-start(f32[128,128]{1,0:T(8,128)S(1)} %slice.171), channel_id=1, source_target_pairs={{8,0},{16,8},{24,16},{9,1},{17,9},{25,17},{10,2},{18,10},{26,18},{... | collective-permute-start | bytes 196616 | tf_op jit(solution)/shard_map/while/body/eval_jaxpr/ppermute | solution.py:15
  414.8 19.9 %collective-permute-start.1 = (f32[128,128]{1,0:T(8,128)S(1)}, f32[128,128]{1,0:T(8,128)S(1)}, u32[]{:S(2)}, u32[]{:S(2)}) collective-permute-start(f32[128,128]{1,0:T(8,128)S(1)} %get-tuple-element.384), channel_id=1, source_target_pairs={{0,8},{8,16},{16,24},{1,9},{9,17},{17,25},{2,10},{10,18},{18,26},{... | collective-permute-start | bytes 196616 | tf_op jit(solution)/shard_map/while/body/eval_jaxpr/ppermute | solution.py:15
  434.7 5.7 %collective-permute-start = (f32[128,128]{1,0:T(8,128)S(1)}, f32[128,128]{1,0:T(8,128)S(1)}, u32[]{:S(2)}, u32[]{:S(2)}) collective-permute-start(f32[128,128]{1,0:T(8,128)S(1)} %slice.171), channel_id=1, source_target_pairs={{8,0},{16,8},{24,16},{9,1},{17,9},{25,17},{10,2},{18,10},{26,18},{... | collective-permute-start | bytes 196616 | tf_op jit(solution)/shard_map/while/body/eval_jaxpr/ppermute | solution.py:15
  456.5 3.1 collective-permute-start.1
  459.6 1.0 copy-start
Sparse Core Ops, SparseCore 0:
  51.7 144.3 all-reduce.2
where the time goes:
time: 470 us; the launch traced here: 467 us
  waiting for transfers between devices  252 us (54%)
  starting transfers between devices  76.4 us (16%)
  between operations  53.7 us (11%)
  local copies, waits for them, and re-layouts  31.5 us (7%)
  matrix products  27.3 us (6%)
  loops' own time  23.2 us (5%)
    psum x1, waiting for transfers between devices, spread(): return lax.psum(block, axis)  144 us
    ppermute x20, waiting for transfers between devices, shifted(): return lax.ppermute(block, axis, route)  107 us
    ppermute x20, starting transfers between devices, shifted(): return lax.ppermute(block, axis, route)  76.4 us
    another operation x10, loops' own time, wave_tick(): lax.cond(active, lambda operands: advance(operands[0], operands[1], benea...  22.5 us
    dot_general x16, matrix products, reflect(): jnp.dot(factor, coeffs, precision=best, preferred_element_type=jnp.float32)  16.8 us
    unnamed x78, local copies, waits for them, and re-layouts  16.1 us
    dynamic_update_slice x12, local copies, waits for them, and re-layouts, advance(): current = lax.dynamic_update_slice_in_dim(current, block, start, 0)  11.9 us
  transfers between devices with their start and end apart: 21, of which 21 were waited for; matrix products, arithmetic and copies ran while one was open for 0% of the time, Pallas kernels for 0%

commit v1 on v0

--- a/solution.py
+++ b/solution.py
@@ -6,7 +6,7 @@
 
 def spread(block, axis, source):
     block = jnp.where(lax.axis_index(axis) == source, block, jnp.zeros_like(block))
-    return lax.psum(block, axis)
+    return jnp.sum(lax.all_gather(block, axis), axis=0)
 
 
 def shifted(block, axis, distance):

time: 470 us -> 977 us (2.08)
  blocking collectives: 0 us -> 422 us
  waiting for transfers between devices: 252 us -> 318 us
  other arithmetic: 3.81 us -> 27.4 us
    all_gather x0 -> x16, blocking collectives: none -> 422 us  [spread(): return jnp.sum(lax.all_gather(block, axis), axis=0)]
    all_gather x0 -> x16, waiting for transfers between devices: none -> 202 us  [spread(): return jnp.sum(lax.all_gather(block, axis), axis=0)]
    psum x1 -> x0, waiting for transfers between devices: 144 us -> none  [spread(): return lax.psum(block, axis)]
    reduce_sum x0 -> x32, other arithmetic: none -> 25 us  [spread(): return jnp.sum(lax.all_gather(block, axis), axis=0)]
  transfers between devices with their start and end apart: 21 -> 36, of which waited for: 21 -> 26; matrix products, arithmetic and copies ran while one was open for 0% -> 3% of each run, Pallas kernels for 0% -> 0%
where the time goes in v1:
time: 977 us; the launch traced here: 974 us
  blocking collectives  422 us (43%)
  waiting for transfers between devices  318 us (33%)
  starting transfers between devices  78.7 us (8%)
  between operations  53.9 us (6%)
  other arithmetic  27.4 us (3%)
  matrix products  27.3 us (3%)
  local copies, waits for them, and re-layouts  23.8 us (2%)
  loops' own time  23.7 us (2%)
    all_gather x16, blocking collectives, spread(): return jnp.sum(lax.all_gather(block, axis), axis=0)  422 us
    all_gather x16, waiting for transfers between devices, spread(): return jnp.sum(lax.all_gather(block, axis), axis=0)  202 us
    ppermute x20, waiting for transfers between devices, shifted(): return lax.ppermute(block, axis, route)  108 us
    ppermute x20, starting transfers between devices, shifted(): return lax.ppermute(block, axis, route)  78.1 us
    reduce_sum x32, other arithmetic, spread(): return jnp.sum(lax.all_gather(block, axis), axis=0)  25 us
    another operation x10, loops' own time, wave_tick(): lax.cond(active, lambda operands: advance(operands[0], operands[1], benea...  23 us
  transfers between devices with their start and end apart: 36, of which 26 were waited for; matrix products, arithmetic and copies ran while one was open for 3% of the time, Pallas kernels for 0%

profile of v1, /device:TPU:3, one launch (start us, length us, event | category | flops | bytes accessed | tf_op | source)
XLA Modules:
  0.0 974.2 jit_solution(5201008511222446966)
XLA Ops:
  59.5 26.2 %all-gather.16 = f32[8,1,128,128]{3,2,1,0:T(8,128)S(1)} all-gather(f32[1,1,128,128]{3,2,1,0:T(8,128)S(1)} %get-tuple-element.289), channel_id=18, replica_groups=mesh['row'=4,'col'=8] {'col'}, dimensions={0}, use_global_device_ids=true | all-gather | bytes 589824 | tf_op jit(solution)/shard_map/all_gather | solution.py:9
  85.7 27.4 %all-gather.17 = f32[8,1,128,128]{3,2,1,0:T(8,128)S(1)} all-gather(f32[1,1,128,128]{3,2,1,0:T(8,128)S(1)} %get-tuple-element.288), channel_id=19, replica_groups=mesh['row'=4,'col'=8] {'col'}, dimensions={0}, use_global_device_ids=true | all-gather | bytes 589824 | tf_op jit(solution)/shard_map/all_gather | solution.py:9
  113.1 26.3 %all-gather.18 = f32[8,1,128,128]{3,2,1,0:T(8,128)S(1)} all-gather(f32[1,1,128,128]{3,2,1,0:T(8,128)S(1)} %get-tuple-element.287), channel_id=20, replica_groups=mesh['row'=4,'col'=8] {'col'}, dimensions={0}, use_global_device_ids=true | all-gather | bytes 589824 | tf_op jit(solution)/shard_map/all_gather | solution.py:9
  139.5 26.0 %all-gather.19 = f32[8,1,128,128]{3,2,1,0:T(8,128)S(1)} all-gather(f32[1,1,128,128]{3,2,1,0:T(8,128)S(1)} %get-tuple-element.286), channel_id=21, replica_groups=mesh['row'=4,'col'=8] {'col'}, dimensions={0}, use_global_device_ids=true | all-gather | bytes 589824 | tf_op jit(solution)/shard_map/all_gather | solution.py:9
  165.5 26.2 %all-gather.20 = f32[8,1,128,128]{3,2,1,0:T(8,128)S(1)} all-gather(f32[1,1,128,128]{3,2,1,0:T(8,128)S(1)} %get-tuple-element.285), channel_id=22, replica_groups=mesh['row'=4,'col'=8] {'col'}, dimensions={0}, use_global_device_ids=true | all-gather | bytes 589824 | tf_op jit(solution)/shard_map/all_gather | solution.py:9
  191.8 26.2 %all-gather.21 = f32[8,1,128,128]{3,2,1,0:T(8,128)S(1)} all-gather(f32[1,1,128,128]{3,2,1,0:T(8,128)S(1)} %get-tuple-element.284), channel_id=23, replica_groups=mesh['row'=4,'col'=8] {'col'}, dimensions={0}, use_global_device_ids=true | all-gather | bytes 589824 | tf_op jit(solution)/shard_map/all_gather | solution.py:9
  218.0 27.0 %all-gather.22 = f32[8,1,128,128]{3,2,1,0:T(8,128)S(1)} all-gather(f32[1,1,128,128]{3,2,1,0:T(8,128)S(1)} %get-tuple-element.282), channel_id=24, replica_groups=mesh['row'=4,'col'=8] {'col'}, dimensions={0}, use_global_device_ids=true | all-gather | bytes 589824 | tf_op jit(solution)/shard_map/all_gather | solution.py:9
  245.1 25.5 %all-gather.23 = f32[8,1,128,128]{3,2,1,0:T(8,128)S(1)} all-gather(f32[1,1,128,128]{3,2,1,0:T(8,128)S(1)} %get-tuple-element.281), channel_id=25, replica_groups=mesh['row'=4,'col'=8] {'col'}, dimensions={0}, use_global_device_ids=true | all-gather | bytes 589824 | tf_op jit(solution)/shard_map/all_gather | solution.py:9
  270.5 26.3 %all-gather.24 = f32[8,1,128,128]{3,2,1,0:T(8,128)S(1)} all-gather(f32[1,1,128,128]{3,2,1,0:T(8,128)S(1)} %get-tuple-element.280), channel_id=26, replica_groups=mesh['row'=4,'col'=8] {'col'}, dimensions={0}, use_global_device_ids=true | all-gather | bytes 589824 | tf_op jit(solution)/shard_map/all_gather | solution.py:9
  296.9 26.3 %all-gather.25 = f32[8,1,128,128]{3,2,1,0:T(8,128)S(1)} all-gather(f32[1,1,128,128]{3,2,1,0:T(8,128)S(1)} %get-tuple-element.279), channel_id=27, replica_groups=mesh['row'=4,'col'=8] {'col'}, dimensions={0}, use_global_device_ids=true | all-gather | bytes 589824 | tf_op jit(solution)/shard_map/all_gather | solution.py:9
  323.2 26.0 %all-gather.26 = f32[8,1,128,128]{3,2,1,0:T(8,128)S(1)} all-gather(f32[1,1,128,128]{3,2,1,0:T(8,128)S(1)} %get-tuple-element.278), channel_id=28, replica_groups=mesh['row'=4,'col'=8] {'col'}, dimensions={0}, use_global_device_ids=true | all-gather | bytes 589824 | tf_op jit(solution)/shard_map/all_gather | solution.py:9
  349.2 26.4 %all-gather.27 = f32[8,1,128,128]{3,2,1,0:T(8,128)S(1)} all-gather(f32[1,1,128,128]{3,2,1,0:T(8,128)S(1)} %get-tuple-element.277), channel_id=29, replica_groups=mesh['row'=4,'col'=8] {'col'}, dimensions={0}, use_global_device_ids=true | all-gather | bytes 589824 | tf_op jit(solution)/shard_map/all_gather | solution.py:9
  375.6 26.3 %all-gather.28 = f32[8,1,128,128]{3,2,1,0:T(8,128)S(1)} all-gather(f32[1,1,128,128]{3,2,1,0:T(8,128)S(1)} %get-tuple-element.276), channel_id=30, replica_groups=mesh['row'=4,'col'=8] {'col'}, dimensions={0}, use_global_device_ids=true | all-gather | bytes 589824 | tf_op jit(solution)/shard_map/all_gather | solution.py:9
  402.0 26.5 %all-gather.29 = f32[8,1,128,128]{3,2,1,0:T(8,128)S(1)} all-gather(f32[1,1,128,128]{3,2,1,0:T(8,128)S(1)} %get-tuple-element.275), channel_id=31, replica_groups=mesh['row'=4,'col'=8] {'col'}, dimensions={0}, use_global_device_ids=true | all-gather | bytes 589824 | tf_op jit(solution)/shard_map/all_gather | solution.py:9
  428.5 27.3 %all-gather.30 = f32[8,1,128,128]{3,2,1,0:T(8,128)S(1)} all-gather(f32[1,1,128,128]{3,2,1,0:T(8,128)S(1)} %get-tuple-element.283), channel_id=32, replica_groups=mesh['row'=4,'col'=8] {'col'}, dimensions={0}, use_global_device_ids=true | all-gather | bytes 589824 | tf_op jit(solution)/shard_map/all_gather | solution.py:9
  455.8 26.1 %all-gather.31 = f32[8,1,128,128]{3,2,1,0:T(8,128)S(1)} all-gather(f32[1,1,128,128]{3,2,1,0:T(8,128)S(1)} %get-tuple-element.274), channel_id=33, replica_groups=mesh['row'=4,'col'=8] {'col'}, dimensions={0}, use_global_device_ids=true | all-gather | bytes 589824 | tf_op jit(solution)/shard_map/all_gather | solution.py:9
  483.1 1.3 reduce_sum.288
  484.4 1.3 reduce_sum.289
  485.8 1.3 reduce_sum.290
  488.4 1.3 reduce_sum.292
  491.1 1.3 reduce_sum.294
  492.5 1.3 reduce_sum.295
  493.8 1.3 reduce_sum.296
  495.1 2.0 reduce_sum.297
  497.1 9.7 all-gather.69.cloned.1.call-done
  506.8 1.9 reduce_sum.298
  508.7 39.4 %all-gather.71.cloned.1.call-done = f32[8,1,256,128]{3,2,1,0:T(8,128)} async-done(((f32[1,1,256,128]{3,2,1,0:T(8,128)}), f32[8,1,256,128]{3,2,1,0:T(8,128)}) %all-gather.71.cloned.1.call-update) | async-done | bytes 1048592 | tf_op jit(solution)/shard_map/all_gather | solution.py:9
  548.2 1.9 reduce_sum.299
  550.1 40.7 %all-gather.73.cloned.1.call-done = f32[8,1,256,128]{3,2,1,0:T(8,128)} async-done(((f32[1,1,256,128]{3,2,1,0:T(8,128)}), f32[8,1,256,128]{3,2,1,0:T(8,128)}) %all-gather.73.cloned.1.call-update) | async-done | bytes 1048592 | tf_op jit(solution)/shard_map/all_gather | solution.py:9
  590.8 1.9 reduce_sum.300
  592.7 39.1 %all-gather.75.cloned.1.call-done = f32[8,1,256,128]{3,2,1,0:T(8,128)} async-done(((f32[1,1,256,128]{3,2,1,0:T(8,128)}), f32[8,1,256,128]{3,2,1,0:T(8,128)}) %all-gather.75.cloned.1.call-update) | async-done | bytes 1048592 | tf_op jit(solution)/shard_map/all_gather | solution.py:9
  631.8 1.9 reduce_sum.301
  633.7 39.1 %all-gather.77.cloned.1.call-done = f32[8,1,256,128]{3,2,1,0:T(8,128)} async-done(((f32[1,1,256,128]{3,2,1,0:T(8,128)}), f32[8,1,256,128]{3,2,1,0:T(8,128)}) %all-gather.77.cloned.1.call-update) | async-done | bytes 1048592 | tf_op jit(solution)/shard_map/all_gather | solution.py:9
  672.8 1.9 reduce_sum.302
  680.3 33.5 %all-gather.79.cloned.1.call-done = f32[8,1,256,128]{3,2,1,0:T(8,128)} async-done(((f32[1,1,256,128]{3,2,1,0:T(8,128)}), f32[8,1,256,128]{3,2,1,0:T(8,128)}) %all-gather.79.cloned.1.call-update) | async-done | bytes 1048592 | tf_op jit(solution)/shard_map/all_gather | solution.py:9
  715.1 251.6 %while.20 = (s32[]{:T(128)}, f32[2048,128]{1,0:T(8,128)S(1)}, f32[128,128]{1,0:T(8,128)S(1)}, s32[]{:T(128)}, s32[1,4,3]{1,0,2:T(1,128)S(1)}, /*index=5*/f32[4,4...) while((s32[]{:T(128)}, f32[2048,128]{1,0:T(8,128)S(1)}, ...), condition=%wide.region_35.36_spmd, body=%wide.region_32.35_spmd.sunk | while | flops 503545888 | bytes 6030164 | solution.py:108
  715.1 4.3 collective-permute-start
  721.6 2.4 collective-permute-done.1
  724.0 4.9 collective-permute-start
  731.0 14.8 %collective-permute-done.1 = f32[128,128]{1,0:T(8,128)S(1)} collective-permute-done((f32[128,128]{1,0:T(8,128)S(1)}, f32[128,128]{1,0:T(8,128)S(1)}, u32[]{:S(2)}, u32[]{:S(2)}) %collective-permute-start.1) | collective-permute-done | bytes 65568 | tf_op jit(solution)/shard_map/while/body/eval_jaxpr/ppermute | solution.py:15
  745.8 20.8 %collective-permute-start = (f32[128,128]{1,0:T(8,128)S(1)}, f32[128,128]{1,0:T(8,128)S(1)}, u32[]{:S(2)}, u32[]{:S(2)}) collective-permute-start(f32[128,128]{1,0:T(8,128)S(1)} %slice.171), channel_id=1, source_target_pairs={{8,0},{16,8},{24,16},{9,1},{17,9},{25,17},{10,2},{18,10},{26,18},{... | collective-permute-start | bytes 196616 | tf_op jit(solution)/shard_map/while/body/eval_jaxpr/ppermute | solution.py:15
  768.8 18.7 %collective-permute-done.1 = f32[128,128]{1,0:T(8,128)S(1)} collective-permute-done((f32[128,128]{1,0:T(8,128)S(1)}, f32[128,128]{1,0:T(8,128)S(1)}, u32[]{:S(2)}, u32[]{:S(2)}) %collective-permute-start.1) | collective-permute-done | bytes 65568 | tf_op jit(solution)/shard_map/while/body/eval_jaxpr/ppermute | solution.py:15
  787.5 4.8 collective-permute-start
  793.3 16.3 %conditional.2 = (f32[2048,128]{1,0:T(8,128)S(1)}, f32[128,128]{1,0:T(8,128)S(1)}) conditional(s32[]{:T(128)} %convert_element_type.11, f32[2048,128]{1,0:T(8,128)S(1)} %get-tuple-element.370, (s32[]{:T(128)}, f32[2048,128]{1,0:T(8,128)S(1)}, f32[128,128]{1,0:T(8,128)S(1)}, s32[]{:T(128)}, s32[1,4,3]{1,0,2:T(1,128)S(1)}, ...), branch_computations={%region_33.33_spmd, %region_34.34_spmd} | conditional | flops 503545856 | bytes 5374306 | solution.py:89
  809.6 1.3 collective-permute-start.1
  810.9 1.8 collective-permute-done.1
  812.7 5.1 collective-permute-start
  820.0 18.7 %collective-permute-done.1 = f32[128,128]{1,0:T(8,128)S(1)} collective-permute-done((f32[128,128]{1,0:T(8,128)S(1)}, f32[128,128]{1,0:T(8,128)S(1)}, u32[]{:S(2)}, u32[]{:S(2)}) %collective-permute-start.1) | collective-permute-done | bytes 65568 | tf_op jit(solution)/shard_map/while/body/eval_jaxpr/ppermute | solution.py:15
  838.7 4.8 collective-permute-start
  844.4 16.2 %conditional.2 = (f32[2048,128]{1,0:T(8,128)S(1)}, f32[128,128]{1,0:T(8,128)S(1)}) conditional(s32[]{:T(128)} %convert_element_type.11, f32[2048,128]{1,0:T(8,128)S(1)} %get-tuple-element.370, (s32[]{:T(128)}, f32[2048,128]{1,0:T(8,128)S(1)}, f32[128,128]{1,0:T(8,128)S(1)}, s32[]{:T(128)}, s32[1,4,3]{1,0,2:T(1,128)S(1)}, ...), branch_computations={%region_33.33_spmd, %region_34.34_spmd} | conditional | flops 503545856 | bytes 5374306 | solution.py:89
  860.6 1.3 collective-permute-start.1
  861.9 1.8 collective-permute-done.1
  863.8 5.4 collective-permute-start
  871.4 18.7 %collective-permute-done.1 = f32[128,128]{1,0:T(8,128)S(1)} collective-permute-done((f32[128,128]{1,0:T(8,128)S(1)}, f32[128,128]{1,0:T(8,128)S(1)}, u32[]{:S(2)}, u32[]{:S(2)}) %collective-permute-start.1) | collective-permute-done | bytes 65568 | tf_op jit(solution)/shard_map/while/body/eval_jaxpr/ppermute | solution.py:15
  890.1 4.8 collective-permute-start
  895.8 16.3 %conditional.2 = (f32[2048,128]{1,0:T(8,128)S(1)}, f32[128,128]{1,0:T(8,128)S(1)}) conditional(s32[]{:T(128)} %convert_element_type.11, f32[2048,128]{1,0:T(8,128)S(1)} %get-tuple-element.370, (s32[]{:T(128)}, f32[2048,128]{1,0:T(8,128)S(1)}, f32[128,128]{1,0:T(8,128)S(1)}, s32[]{:T(128)}, s32[1,4,3]{1,0,2:T(1,128)S(1)}, ...), branch_computations={%region_33.33_spmd, %region_34.34_spmd} | conditional | flops 503545856 | bytes 5374306 | solution.py:89
  912.2 1.3 collective-permute-start.1
  913.5 1.8 collective-permute-done.1
  915.3 5.4 collective-permute-start
  922.9 18.7 %collective-permute-done.1 = f32[128,128]{1,0:T(8,128)S(1)} collective-permute-done((f32[128,128]{1,0:T(8,128)S(1)}, f32[128,128]{1,0:T(8,128)S(1)}, u32[]{:S(2)}, u32[]{:S(2)}) %collective-permute-start.1) | collective-permute-done | bytes 65568 | tf_op jit(solution)/shard_map/while/body/eval_jaxpr/ppermute | solution.py:15
  941.6 4.8 collective-permute-start
  947.3 16.2 %conditional.2 = (f32[2048,128]{1,0:T(8,128)S(1)}, f32[128,128]{1,0:T(8,128)S(1)}) conditional(s32[]{:T(128)} %convert_element_type.11, f32[2048,128]{1,0:T(8,128)S(1)} %get-tuple-element.370, (s32[]{:T(128)}, f32[2048,128]{1,0:T(8,128)S(1)}, f32[128,128]{1,0:T(8,128)S(1)}, s32[]{:T(128)}, s32[1,4,3]{1,0,2:T(1,128)S(1)}, ...), branch_computations={%region_33.33_spmd, %region_34.34_spmd} | conditional | flops 503545856 | bytes 5374306 | solution.py:89
  963.6 1.3 collective-permute-start.1
  964.9 1.8 collective-permute-done.1
  (227 shorter events, 83.1 us)
Async XLA Ops:
  6.5 18.9 %copy-start.2 = (f32[1,4,256,128]{3,2,1,0:T(8,128)S(1)}, f32[1,4,256,128]{3,2,1,0:T(8,128)}, u32[]{:S(2)}) copy-start(f32[1,4,256,128]{3,2,1,0:T(8,128)} %param.10) | copy-start | bytes 1572868
  6.5 0.7 copy-start.6
  6.5 475.6 %all-gather.49.cloned.1.call-start = ((), (), s32[]{:S(2)}) async-start(), calls=%async_computation | async-start | bytes 1179648 | tf_op jit(solution)/shard_map/all_gather | solution.py:9
  26.4 458.0 %all-gather.51.cloned.1.call-start = ((), (), s32[]{:S(2)}) async-start(), calls=%async_computation.1 | async-start | bytes 1179648 | tf_op jit(solution)/shard_map/all_gather | solution.py:9
  27.2 458.6 %all-gather.53.cloned.1.call-start = ((), (), s32[]{:S(2)}) async-start(), calls=%async_computation.2 | async-start | bytes 1179648 | tf_op jit(solution)/shard_map/all_gather | solution.py:9
  27.9 459.2 %all-gather.55.cloned.1.call-start = ((), (), s32[]{:S(2)}) async-start(), calls=%async_computation.3 | async-start | bytes 1179648 | tf_op jit(solution)/shard_map/all_gather | solution.py:9
  28.5 460.0 %all-gather.57.cloned.1.call-start = ((), (), s32[]{:S(2)}) async-start(), calls=%async_computation.4 | async-start | bytes 1179648 | tf_op jit(solution)/shard_map/all_gather | solution.py:9
  29.1 460.7 %all-gather.59.cloned.1.call-start = ((), (), s32[]{:S(2)}) async-start(), calls=%async_computation.5 | async-start | bytes 1179648 | tf_op jit(solution)/shard_map/all_gather | solution.py:9
  29.6 29.7 %copy-start.3 = (f32[1,4,128,128]{3,2,1,0:T(8,128)S(1)}, f32[1,4,128,128]{3,2,1,0:T(8,128)}, u32[]{:S(2)}) copy-start(f32[1,4,128,128]{3,2,1,0:T(8,128)} %param.11) | copy-start | bytes 786436
  29.7 461.5 %all-gather.61.cloned.1.call-start = ((), (), s32[]{:S(2)}) async-start(), calls=%async_computation.6 | async-start | bytes 1179648 | tf_op jit(solution)/shard_map/all_gather | solution.py:9
  53.5 439.0 %all-gather.63.cloned.1.call-start = ((), (), s32[]{:S(2)}) async-start(), calls=%async_computation.7 | async-start | bytes 1179648 | tf_op jit(solution)/shard_map/all_gather | solution.py:9
  54.2 439.6 %all-gather.65.cloned.1.call-start = ((), (), s32[]{:S(2)}) async-start(), calls=%async_computation.8 | async-start | bytes 1179648 | tf_op jit(solution)/shard_map/all_gather | solution.py:9
  54.9 440.2 %all-gather.67.cloned.1.call-start = ((), (), s32[]{:S(2)}) async-start(), calls=%async_computation.9 | async-start | bytes 1179648 | tf_op jit(solution)/shard_map/all_gather | solution.py:9
  55.5 451.3 %all-gather.69.cloned.1.call-start = ((), (), s32[]{:S(2)}) async-start(), calls=%async_computation.10 | async-start | bytes 1179648 | tf_op jit(solution)/shard_map/all_gather | solution.py:9
  56.3 491.9 %all-gather.71.cloned.1.call-start = ((), (), s32[]{:S(2)}) async-start(), calls=%async_computation.11 | async-start | bytes 1179648 | tf_op jit(solution)/shard_map/all_gather | solution.py:9
  56.8 533.9 %all-gather.73.cloned.1.call-start = ((), (), s32[]{:S(2)}) async-start(), calls=%async_computation.12 | async-start | bytes 1179648 | tf_op jit(solution)/shard_map/all_gather | solution.py:9
  57.6 574.2 %all-gather.75.cloned.1.call-start = ((), (), s32[]{:S(2)}) async-start(), calls=%async_computation.13 | async-start | bytes 1179648 | tf_op jit(solution)/shard_map/all_gather | solution.py:9
  58.2 614.6 %all-gather.77.cloned.1.call-start = ((), (), s32[]{:S(2)}) async-start(), calls=%async_computation.14 | async-start | bytes 1179648 | tf_op jit(solution)/shard_map/all_gather | solution.py:9
  58.8 655.0 %all-gather.79.cloned.1.call-start = ((), (), s32[]{:S(2)}) async-start(), calls=%async_computation.15 | async-start | bytes 1179648 | tf_op jit(solution)/shard_map/all_gather | solution.py:9
  482.1 1.0 copy-start.4
  674.7 40.4 %copy-start.1 = (f32[2048,128]{1,0:T(8,128)S(1)}, f32[2048,128]{1,0:T(8,128)}, u32[]{:S(2)}) copy-start(f32[2048,128]{1,0:T(8,128)} %param.9) | copy-start | bytes 3145732
  674.7 40.4 %copy-start.5 = (s32[1,4,3]{1,0,2:T(1,128)S(1)}, s32[1,4,3]{1,0,2:T(1,128)}, u32[]{:S(2)}) copy-start(s32[1,4,3]{1,0,2:T(1,128)} %param.13) | copy-start | bytes 148
  715.1 5.2 collective-permute-start
  720.3 3.7 collective-permute-start.1
  724.0 5.8 collective-permute-start
  729.8 16.1 %collective-permute-start.1 = (f32[128,128]{1,0:T(8,128)S(1)}, f32[128,128]{1,0:T(8,128)S(1)}, u32[]{:S(2)}, u32[]{:S(2)}) collective-permute-start(f32[128,128]{1,0:T(8,128)S(1)} %get-tuple-element.352), channel_id=1, source_target_pairs={{0,8},{8,16},{16,24},{1,9},{9,17},{17,25},{2,10},{10,18},{18,26},{... | collective-permute-start | bytes 196616 | tf_op jit(solution)/shard_map/while/body/eval_jaxpr/ppermute | solution.py:15
  745.8 21.7 %collective-permute-start = (f32[128,128]{1,0:T(8,128)S(1)}, f32[128,128]{1,0:T(8,128)S(1)}, u32[]{:S(2)}, u32[]{:S(2)}) collective-permute-start(f32[128,128]{1,0:T(8,128)S(1)} %slice.171), channel_id=1, source_target_pairs={{8,0},{16,8},{24,16},{9,1},{17,9},{25,17},{10,2},{18,10},{26,18},{... | collective-permute-start | bytes 196616 | tf_op jit(solution)/shard_map/while/body/eval_jaxpr/ppermute | solution.py:15
  767.5 20.0 %collective-permute-start.1 = (f32[128,128]{1,0:T(8,128)S(1)}, f32[128,128]{1,0:T(8,128)S(1)}, u32[]{:S(2)}, u32[]{:S(2)}) collective-permute-start(f32[128,128]{1,0:T(8,128)S(1)} %get-tuple-element.352), channel_id=1, source_target_pairs={{0,8},{8,16},{16,24},{1,9},{9,17},{17,25},{2,10},{10,18},{18,26},{... | collective-permute-start | bytes 196616 | tf_op jit(solution)/shard_map/while/body/eval_jaxpr/ppermute | solution.py:15
  787.5 5.7 collective-permute-start
  809.6 3.1 collective-permute-start.1
  812.7 6.0 collective-permute-start
  818.7 20.0 %collective-permute-start.1 = (f32[128,128]{1,0:T(8,128)S(1)}, f32[128,128]{1,0:T(8,128)S(1)}, u32[]{:S(2)}, u32[]{:S(2)}) collective-permute-start(f32[128,128]{1,0:T(8,128)S(1)} %get-tuple-element.352), channel_id=1, source_target_pairs={{0,8},{8,16},{16,24},{1,9},{9,17},{17,25},{2,10},{10,18},{18,26},{... | collective-permute-start | bytes 196616 | tf_op jit(solution)/shard_map/while/body/eval_jaxpr/ppermute | solution.py:15
  838.7 5.7 collective-permute-start
  860.6 3.1 collective-permute-start.1
  863.8 6.3 collective-permute-start
  870.1 20.0 %collective-permute-start.1 = (f32[128,128]{1,0:T(8,128)S(1)}, f32[128,128]{1,0:T(8,128)S(1)}, u32[]{:S(2)}, u32[]{:S(2)}) collective-permute-start(f32[128,128]{1,0:T(8,128)S(1)} %get-tuple-element.352), channel_id=1, source_target_pairs={{0,8},{8,16},{16,24},{1,9},{9,17},{17,25},{2,10},{10,18},{18,26},{... | collective-permute-start | bytes 196616 | tf_op jit(solution)/shard_map/while/body/eval_jaxpr/ppermute | solution.py:15
  890.1 5.7 collective-permute-start
  912.2 3.1 collective-permute-start.1
  915.3 6.3 collective-permute-start
  921.6 20.0 %collective-permute-start.1 = (f32[128,128]{1,0:T(8,128)S(1)}, f32[128,128]{1,0:T(8,128)S(1)}, u32[]{:S(2)}, u32[]{:S(2)}) collective-permute-start(f32[128,128]{1,0:T(8,128)S(1)} %get-tuple-element.352), channel_id=1, source_target_pairs={{0,8},{8,16},{16,24},{1,9},{9,17},{17,25},{2,10},{10,18},{18,26},{... | collective-permute-start | bytes 196616 | tf_op jit(solution)/shard_map/while/body/eval_jaxpr/ppermute | solution.py:15
  941.6 5.7 collective-permute-start
  963.6 3.1 collective-permute-start.1
  966.7 1.0 copy-start
Sparse Core Ops, SparseCore 0:
  26.5 40.5 all-gather.48
  69.2 41.8 all-gather.50
  113.2 42.7 all-gather.52
  158.0 41.1 all-gather.54
  201.2 42.9 all-gather.56
  246.1 42.7 all-gather.58
  291.0 42.4 all-gather.60
  335.7 39.1 all-gather.62
  377.0 43.6 all-gather.64
  422.7 41.4 all-gather.66
  466.3 40.4 all-gather.68
  508.8 39.3 all-gather.70
  550.3 40.4 all-gather.72
  592.7 38.9 all-gather.74
  633.7 38.9 all-gather.76
  674.7 38.9 all-gather.78
